TPU v7x, 32 devices: a whole 2x2x4 slice. The times are simulated.
32 devices in a mesh: groups: 2 (over x), dp: 16 (over z, y, core).
Axes of the slice: x: 2, y: 2, z: 4, core: 2. Of those that a mesh axis runs over, the one named last changes fastest.
Arguments:
- states: bfloat16 [16384, 1024], P(('groups', 'dp')), parts along dimension 0, may hold values from -6 to 6
- lengths: int32 [64], P(('groups', 'dp')), parts along dimension 0, may hold values from 1 to 256, as said below
- norm_gain: bfloat16 [1024], replicated, may hold values from 0.5 to 2
- w_gate: bfloat16 [1024, 1536], replicated, may hold values from -0.1875 to 0.1875
- w_up: bfloat16 [1024, 1536], replicated, may hold values from -0.1875 to 0.1875
- w_down: bfloat16 [1536, 1024], replicated, may hold values from -0.15625 to 0.15625
- context: bfloat16 [64, 4096], P('groups', 'dp'), parts along dimension 0, may hold values from -6 to 6
- w_out: bfloat16 [4096, 4096], P('dp'), may hold values from -0.09375 to 0.09375
- resid_stream: bfloat16 [64, 4096], P('groups'), parts along dimension 0, may hold values from -6 to 6
- teacher_gain: bfloat16 [4096], replicated, may hold values from 0.5 to 2
Outputs:
- gram_loss: float32 [2], P('groups'), parts along dimension 0
- grad_gate: float32 [2048, 1536], P(('groups', 'dp')), parts along dimension 0
- grad_up: float32 [2048, 1536], P(('groups', 'dp')), parts along dimension 0
- grad_down: float32 [3072, 1024], P(('groups', 'dp')), parts along dimension 0
There are 2 independent parts, one for each index of `groups`. A program takes and returns all parts, laid end to end along the dimension named above; an argument that names none is the same for every part. Nothing has to cross between parts.
Inputs may be any that keep to these rules, and one draw needn't show every extreme that they name: `lengths`: some document of every group fills all 256 slots and some has a single valid token.
All inputs are finite; a program needn't handle non-finite values.
Results may differ from a plain program's by a relative error of at most 0.004.
Values may be sent and summed in bfloat16 or wider, within the bound.
A program may use at most 128 MiB of HBM per device.

v0:
```python
import jax
import jax.numpy as jnp
from jax import lax
from jax.sharding import PartitionSpec as P

EPS = 1e-06
LOSS_SCALE = 4096.0


def teacher_embed(attn_rows, resid_rows, teacher_gain):
    scaled_rows = teacher_gain.astype(jnp.float32) * (resid_rows.astype(jnp.float32) + attn_rows)
    inv_teacher = lax.rsqrt(jnp.sum(scaled_rows * scaled_rows, axis=1, keepdims=True) + EPS)
    return (scaled_rows * inv_teacher).astype(jnp.bfloat16)


def rows_product(left_rows, right_rows):
    return lax.dot_general(
        left_rows, right_rows, (((1,), (1,)), ((), ())), preferred_element_type=jnp.float32
    )


def cols_product(left_cols, right_cols):
    return lax.dot_general(
        left_cols, right_cols, (((0,), (0,)), ((), ())), preferred_element_type=jnp.float32
    )


def per_device(
    states, lengths, norm_gain, w_gate, w_up, w_down, context, w_out, resid_stream, teacher_gain
):
    my_index = lax.axis_index("dp")
    doc_dev = lengths.shape[0]
    seq_len = states.shape[0] // doc_dev
    model_width = states.shape[1]
    hidden_width = w_gate.shape[1]
    first_doc = my_index * doc_dev
    partial_attn = jnp.dot(context, w_out, preferred_element_type=jnp.float32)
    attn_own = lax.psum_scatter(partial_attn, "dp", scatter_dimension=0, tiled=True)
    resid_own = lax.dynamic_slice_in_dim(resid_stream, first_doc, doc_dev, 0)
    teacher_own = teacher_embed(attn_own, resid_own, teacher_gain)
    teacher_all = lax.all_gather(teacher_own, "dp", axis=0, tiled=True)
    gram_rows = rows_product(teacher_own, teacher_all)
    teacher_square = jnp.sum(gram_rows * gram_rows)
    states_wide = states.astype(jnp.float32)
    inv_rms = lax.rsqrt(jnp.mean(states_wide * states_wide, axis=1, keepdims=True) + EPS)
    normed = (states_wide * inv_rms * norm_gain.astype(jnp.float32)).astype(jnp.bfloat16)
    gate_pre = jnp.dot(normed, w_gate, preferred_element_type=jnp.float32)
    up_pre = jnp.dot(normed, w_up, preferred_element_type=jnp.float32)
    hidden = (jax.nn.silu(gate_pre) * up_pre).astype(jnp.bfloat16)
    layer_out = states_wide + jnp.dot(hidden, w_down, preferred_element_type=jnp.float32)
    positions = lax.broadcasted_iota(jnp.int32, (doc_dev, seq_len), 1)
    valid_mask = (positions < lengths[:, None]).astype(jnp.float32)
    counts = lengths.astype(jnp.float32)
    pooled = (
        jnp.sum(layer_out.reshape(doc_dev, seq_len, model_width) * valid_mask[:, :, None], axis=1)
        / counts[:, None]
    )
    inv_norm = lax.rsqrt(jnp.sum(pooled * pooled, axis=1, keepdims=True) + EPS)
    unit_rows = pooled * inv_norm
    embed_own = unit_rows.astype(jnp.bfloat16)
    embed_all = lax.all_gather(embed_own, "dp", axis=0, tiled=True)
    student_rows = rows_product(embed_own, embed_all)
    gram_diff = student_rows - gram_rows
    diff_square = jnp.sum(gram_diff * gram_diff)
    total_diff, total_teacher = lax.psum((diff_square, teacher_square), "dp")
    diff_norm = jnp.sqrt(total_diff + EPS)
    teacher_norm = jnp.sqrt(total_teacher)
    gram_loss = (diff_norm / teacher_norm).reshape(1)
    d_gram = LOSS_SCALE * gram_diff / (diff_norm * teacher_norm)
    d_embed = 2.0 * jnp.dot(d_gram, embed_all.astype(jnp.float32), precision=lax.Precision.HIGHEST)
    along = jnp.sum(unit_rows * d_embed, axis=1, keepdims=True)
    d_pooled = (d_embed - unit_rows * along) * inv_norm
    d_doc = (d_pooled / counts[:, None]).astype(jnp.bfloat16)
    d_hidden = rows_product(d_doc, w_down)
    d_hidden_tok = (d_hidden[:, None, :] * valid_mask[:, :, None]).reshape(
        doc_dev * seq_len, hidden_width
    )
    sigmoid_gate = jax.nn.sigmoid(gate_pre)
    d_gate = (
        d_hidden_tok * up_pre * sigmoid_gate * (1.0 + gate_pre * (1.0 - sigmoid_gate))
    ).astype(jnp.bfloat16)
    d_up = (d_hidden_tok * jax.nn.silu(gate_pre)).astype(jnp.bfloat16)
    term_gate = cols_product(normed, d_gate)
    term_up = cols_product(normed, d_up)
    d_token = (
        (d_doc.astype(jnp.float32)[:, None, :] * valid_mask[:, :, None])
        .astype(jnp.bfloat16)
        .reshape(doc_dev * seq_len, model_width)
    )
    term_down = cols_product(hidden, d_token)
    grad_gate, grad_up, grad_down = (
        lax.psum_scatter(term_gate, "dp", scatter_dimension=0, tiled=True),
        lax.psum_scatter(term_up, "dp", scatter_dimension=0, tiled=True),
        lax.psum_scatter(term_down, "dp", scatter_dimension=0, tiled=True),
    )
    return (gram_loss, grad_gate, grad_up, grad_down)


def solution(mesh):
    in_specs = (
        P(("groups", "dp"), None),
        P(("groups", "dp")),
        P(),
        P(),
        P(),
        P(),
        P("groups", "dp"),
        P("dp", None),
        P("groups", None),
        P(),
    )
    out_specs = (
        P("groups"),
        P(("groups", "dp"), None),
        P(("groups", "dp"), None),
        P(("groups", "dp"), None),
    )
    return jax.shard_map(
        per_device, mesh=mesh, in_specs=in_specs, out_specs=out_specs, check_vma=False
    )
```

profile of v0, /device:TPU:0, one launch (start us, length us, event | category | flops | bytes accessed | tf_op | source)
XLA Modules:
  0.0 443.4 jit_solution(15152282019236517308)
XLA Ops:
  7.2 3.1 fusion.30
  10.3 0.0 reduce-scatter.4.cloned.1.call-start
  10.4 0.1 fusion.18
  10.5 1.5 fusion.7
  12.0 4.2 fusion.25
  16.2 3.7 multiply_convert_fusion
  19.9 1.8 multiply_reduce_fusion
  21.8 0.2 multiply_reduce_fusion.3
  22.0 0.1 fusion.50
  22.1 23.3 %all-gather = bf16[16,2,1024]{2,1,0:T(2,128)(2,1)S(1)} all-gather(bf16[1,2,1024]{2,1,0:T(2,128)(2,1)S(1)} %fusion.50), channel_id=1, replica_groups=mesh['groups'=2,'dp'=16] {'dp'}, dimensions={0}, use_global_device_ids=true | all-gather | bytes 69632 | tf_op jit(solution)/shard_map/all_gather | solution.py:61
  45.5 0.6 dynamic-slice
  46.7 57.6 %all-reduce.4.cloned.1.call-done = f32[32,4096]{1,0:T(8,128)} async-done(((f32[32,4096]{1,0:T(8,128)}), f32[32,4096]{1,0:T(8,128)}) %all-reduce.4.cloned.1.call-update) | async-done | bytes 524304
  104.3 1.1 multiply_reduce_fusion.1
  105.4 0.1 fusion.51
  105.5 21.5 %all-gather.1 = bf16[16,2,4096]{2,1,0:T(2,128)(2,1)S(1)} all-gather(bf16[1,2,4096]{2,1,0:T(2,128)(2,1)S(1)} %fusion.51), channel_id=1, replica_groups=mesh['groups'=2,'dp'=16] {'dp'}, dimensions={0}, use_global_device_ids=true | all-gather | bytes 278528 | tf_op jit(solution)/shard_map/all_gather | solution.py:41
  127.0 0.8 reshape.79
  127.8 1.8 multiply_reduce_fusion.4
  129.6 0.8 multiply_reduce_fusion.5
  130.4 30.4 %all-reduce.1 = (f32[]{:T(128)}, f32[]{:T(128)}) all-reduce(f32[]{:T(128)} %get-tuple-element.18, f32[]{:T(128)} %get-tuple-element.20), channel_id=1, replica_groups=mesh['groups'=2,'dp'=16] {'dp'}, use_global_device_ids=true, to_apply=%region_6.7 | all-reduce | flops 2 | bytes 16 | tf_op jit(solution)/shard_map/psum | solution.py:65
  162.2 0.3 multiply_reduce_fusion.2
  162.5 0.1 fusion.27
  162.6 3.0 fusion.31
  165.6 4.4 fusion.5
  170.0 4.6 %fusion.21 = f32[1024,1536]{1,0:T(8,128)} fusion(bf16[512,1536]{1,0:T(8,128)(2,1)S(1)} %get-tuple-element.13, bf16[512,1024]{1,0:T(8,128)(2,1)S(1)} %copy-done.5, f32[1024]{0:T(1024)S(1)} %convert_element_type.58, f32[512]{0:T(512)S(1)} %add_rsqrt_fusion), kind=kOutput, calls=%fused_computation.44 | convolution fusion | flops 1612709888 | bytes 8919040 | tf_op jit(solution)/shard_map/dot_general | solution.py:23
  174.6 0.0 reduce-scatter.6.cloned.1.call-start
  174.7 6.3 %fusion.19 = f32[1024,1536]{1,0:T(8,128)} fusion(bf16[512,1536]{1,0:T(8,128)(2,1)} %get-tuple-element.12, bf16[512,1024]{1,0:T(8,128)(2,1)} %param.10, f32[1024]{0:T(1024)S(1)} %convert_element_type.58, f32[512]{0:T(512)S(1)} %add_rsqrt_fusion), kind=kOutput, calls=%fused_computation.43 | convolution fusion | flops 1612709888 | bytes 8919040 | tf_op jit(solution)/shard_map/dot_general | solution.py:23
  181.0 0.0 reduce-scatter.8.cloned.1.call-start
  181.1 0.2 fusion.10
  181.3 6.0 %fusion.32 = f32[1536,1024]{1,0:T(8,128)} fusion(bf16[512,1536]{1,0:T(8,128)(2,1)} %copy-done.10, bf16[512,1024]{1,0:T(8,128)(2,1)S(1)} %fusion.10), kind=kOutput, calls=%fused_computation.50 | convolution fusion | flops 1610612736 | bytes 8912896 | tf_op jit(solution)/shard_map/dot_general | solution.py:23
  187.3 69.8 %reduce-scatter.4.cloned.1.call-done = f32[64,1536]{1,0:T(8,128)} async-done(((f32[1024,1536]{1,0:T(8,128)}), f32[64,1536]{1,0:T(8,128)}) %reduce-scatter.4.cloned.1.call-update) | async-done | bytes 393232 | tf_op jit(solution)/shard_map/reduce_scatter | solution.py:92
  257.2 89.6 %reduce-scatter.6.cloned.1.call-done = f32[64,1536]{1,0:T(8,128)} async-done(((f32[1024,1536]{1,0:T(8,128)}), f32[64,1536]{1,0:T(8,128)}) %reduce-scatter.6.cloned.1.call-update) | async-done | bytes 393232 | tf_op jit(solution)/shard_map/reduce_scatter | solution.py:93
  346.8 88.9 %reduce-scatter.8.cloned.1.call-done = f32[96,1024]{1,0:T(8,128)} async-done(((f32[1536,1024]{1,0:T(8,128)}), f32[96,1024]{1,0:T(8,128)}) %reduce-scatter.8.cloned.1.call-update) | async-done | bytes 393232 | tf_op jit(solution)/shard_map/reduce_scatter | solution.py:94
  (35 shorter events, 0.2 us)
Async XLA Ops:
  7.2 9.0 %copy-start = (bf16[1024,1536]{1,0:T(8,128)(2,1)S(1)}, bf16[1024,1536]{1,0:T(8,128)(2,1)}, u32[]{:S(2)}) copy-start(bf16[1024,1536]{1,0:T(8,128)(2,1)} %param.14) | copy-start | bytes 9437188
  7.2 3.2 copy-start.8
  7.2 3.3 copy-start.7
  7.2 97.1 %all-reduce.4.cloned.1.call-start = ((), (), s32[]{:S(2)}) async-start(), calls=%async_computation.6 | async-start | bytes 1048576
  10.3 246.9 %reduce-scatter.4.cloned.1.call-start = ((), (), s32[]{:S(2)}) async-start(), calls=%async_computation.3 | async-start | bytes 6684672 | tf_op jit(solution)/shard_map/reduce_scatter | solution.py:92
  12.0 4.2 copy-start.4
  16.2 3.7 copy-start.2
  16.2 3.7 copy-start.1
  19.9 1.9 copy-start.10
  19.9 2.1 copy-start.6
  19.9 25.5 %copy-start.9 = (u32[32]{0:T(128)S(1)}, u32[32]{0:T(128)}, u32[]{:S(2)}) copy-start(u32[32]{0:T(128)} %constant.31) | copy-start | bytes 388
  162.2 3.4 copy-start.3
  165.6 4.4 copy-start.5
  174.6 172.2 %reduce-scatter.6.cloned.1.call-start = ((), (), s32[]{:S(2)}) async-start(), calls=%async_computation.4 | async-start | bytes 6684672 | tf_op jit(solution)/shard_map/reduce_scatter | solution.py:93
  181.0 254.7 %reduce-scatter.8.cloned.1.call-start = ((), (), s32[]{:S(2)}) async-start(), calls=%async_computation.5 | async-start | bytes 6684672 | tf_op jit(solution)/shard_map/reduce_scatter | solution.py:94
Sparse Core Ops, SparseCore 0:
  11.4 92.8 all-reduce.3
  174.7 82.4 reduce-scatter.3
  262.2 84.5 reduce-scatter.5
  351.1 84.5 reduce-scatter.7
where the time goes:
time: 444 us; the launch traced here: 443 us
  waiting for transfers between devices  306 us (69%)
  blocking collectives  75.3 us (17%)
  matrix products  35.5 us (8%)
  between operations  17.2 us (4%)
  other arithmetic  7.69 us (2%)
    reduce_scatter x1, waiting for transfers between devices, per_device(): lax.psum_scatter(term_up, 'dp', scatter_dimension=0, tiled=True)  89.6 us
    reduce_scatter x1, waiting for transfers between devices, per_device(): lax.psum_scatter(term_down, 'dp', scatter_dimension=0, tiled=True)  88.9 us
    reduce_scatter x1, waiting for transfers between devices, per_device(): lax.psum_scatter(term_gate, 'dp', scatter_dimension=0, tiled=True)  69.8 us
    unnamed x5, waiting for transfers between devices  57.7 us
    psum x1, blocking collectives, per_device(): total_diff, total_teacher = lax.psum((diff_square, teacher_square), 'dp')  30.4 us
    all_gather x1, blocking collectives, per_device(): embed_all = lax.all_gather(embed_own, 'dp', axis=0, tiled=True)  23.3 us
    all_gather x1, blocking collectives, per_device(): teacher_all = lax.all_gather(teacher_own, 'dp', axis=0, tiled=True)  21.5 us
    dot_general x3, matrix products, cols_product(): lax.dot_general(left_cols, right_cols, (((0,), (0,)), ((), ())), preferre...  16.9 us
  transfers between devices with their start and end apart: 4, of which 4 were waited for; matrix products, arithmetic and copies ran while one was open for 6% of the time, Pallas kernels for 0%

commit v1 on v0

v1 whole, which is shorter than its diff:
```python
import jax
import jax.numpy as jnp
from jax import lax
from jax.sharding import PartitionSpec as P

EPS = 1e-06
LOSS_SCALE = 4096.0


def teacher_embed(attn_rows, resid_rows, teacher_gain):
    scaled_rows = teacher_gain.astype(jnp.float32) * (resid_rows.astype(jnp.float32) + attn_rows)
    inv_teacher = lax.rsqrt(jnp.sum(scaled_rows * scaled_rows, axis=1, keepdims=True) + EPS)
    return (scaled_rows * inv_teacher).astype(jnp.bfloat16)


def rows_product(left_rows, right_rows):
    return lax.dot_general(
        left_rows, right_rows, (((1,), (1,)), ((), ())), preferred_element_type=jnp.float32
    )


def cols_product(left_cols, right_cols):
    return lax.dot_general(
        left_cols, right_cols, (((0,), (0,)), ((), ())), preferred_element_type=jnp.float32
    )


def per_device(
    states, lengths, norm_gain, w_gate, w_up, w_down, context, w_out, resid_stream, teacher_gain
):
    dp = lax.axis_size("dp")
    my_index = lax.axis_index("dp")
    doc_dev = lengths.shape[0]
    seq_len = states.shape[0] // doc_dev
    model_width = states.shape[1]
    hidden_width = w_gate.shape[1]
    feat = w_out.shape[1] // dp
    high = lax.Precision.HIGHEST
    partial_attn = jnp.dot(context, w_out, preferred_element_type=jnp.float32)
    attn_cols = lax.psum_scatter(partial_attn, "dp", scatter_dimension=1, tiled=True)
    resid_cols = lax.dynamic_slice_in_dim(resid_stream, my_index * feat, feat, 1)
    gain_cols = lax.dynamic_slice_in_dim(teacher_gain, my_index * feat, feat, 0)
    scaled = gain_cols.astype(jnp.float32) * (resid_cols.astype(jnp.float32) + attn_cols)
    gram_part = lax.dot_general(scaled, scaled, (((1,), (1,)), ((), ())), precision=high)
    states_wide = states.astype(jnp.float32)
    inv_rms = lax.rsqrt(jnp.mean(states_wide * states_wide, axis=1, keepdims=True) + EPS)
    normed = (states_wide * inv_rms * norm_gain.astype(jnp.float32)).astype(jnp.bfloat16)
    gate_pre = jnp.dot(normed, w_gate, preferred_element_type=jnp.float32)
    up_pre = jnp.dot(normed, w_up, preferred_element_type=jnp.float32)
    hidden = (jax.nn.silu(gate_pre) * up_pre).astype(jnp.bfloat16)
    positions = lax.broadcasted_iota(jnp.int32, (doc_dev, seq_len), 1)
    valid_mask = (positions < lengths[:, None]).astype(jnp.float32)
    counts = lengths.astype(jnp.float32)
    hidden_sum = jnp.sum(
        hidden.astype(jnp.float32).reshape(doc_dev, seq_len, hidden_width) * valid_mask[:, :, None], axis=1
    )
    state_sum = jnp.sum(states_wide.reshape(doc_dev, seq_len, model_width) * valid_mask[:, :, None], axis=1)
    packed = jnp.concatenate([hidden_sum, state_sum, jnp.broadcast_to(counts[:, None], (doc_dev, 128))], axis=1)
    packed_all = lax.all_gather(packed, "dp", axis=0, tiled=True)
    hidden_all = packed_all[:, :hidden_width]
    state_all = packed_all[:, hidden_width : hidden_width + model_width]
    count_all = packed_all[:, hidden_width + model_width :][:, :1]
    gram_raw = lax.psum(gram_part, "dp")
    docs = gram_raw.shape[0]
    eye = jnp.eye(docs, dtype=jnp.float32)
    inv_col = lax.rsqrt(jnp.sum(gram_raw * eye, axis=1, keepdims=True) + EPS)
    inv_row = lax.rsqrt(jnp.sum(gram_raw * eye, axis=0, keepdims=True) + EPS)
    gram_teacher = gram_raw * inv_col * inv_row
    pooled = (state_all + jnp.dot(hidden_all, w_down.astype(jnp.float32), precision=high)) / count_all
    inv_norm = lax.rsqrt(jnp.sum(pooled * pooled, axis=1, keepdims=True) + EPS)
    unit_rows = pooled * inv_norm
    embed = unit_rows.astype(jnp.bfloat16)
    gram_diff = rows_product(embed, embed) - gram_teacher
    diff_norm = jnp.sqrt(jnp.sum(gram_diff * gram_diff) + EPS)
    teacher_norm = jnp.sqrt(jnp.sum(gram_teacher * gram_teacher))
    gram_loss = (diff_norm / teacher_norm).reshape(1)
    d_gram = LOSS_SCALE * gram_diff / (diff_norm * teacher_norm)
    d_embed = 2.0 * jnp.dot(d_gram, embed.astype(jnp.float32), precision=high)
    along = jnp.sum(unit_rows * d_embed, axis=1, keepdims=True)
    d_pooled = (d_embed - unit_rows * along) * inv_norm
    d_all = (d_pooled / count_all).astype(jnp.bfloat16)
    down_rows = hidden_width // dp
    own_hidden = lax.dynamic_slice_in_dim(hidden_all, my_index * down_rows, down_rows, 1)
    grad_down = lax.dot_general(
        own_hidden, d_all.astype(jnp.float32), (((0,), (0,)), ((), ())), precision=high
    )
    d_doc = lax.dynamic_slice_in_dim(d_all, my_index * doc_dev, doc_dev, 0)
    d_hidden = rows_product(d_doc, w_down)
    d_hidden_tok = (d_hidden[:, None, :] * valid_mask[:, :, None]).reshape(
        doc_dev * seq_len, hidden_width
    )
    sigmoid_gate = jax.nn.sigmoid(gate_pre)
    d_gate = (
        d_hidden_tok * up_pre * sigmoid_gate * (1.0 + gate_pre * (1.0 - sigmoid_gate))
    ).astype(jnp.bfloat16)
    d_up = (d_hidden_tok * jax.nn.silu(gate_pre)).astype(jnp.bfloat16)
    rows = model_width // dp
    terms = jnp.concatenate([cols_product(normed, d_gate), cols_product(normed, d_up)], axis=1)
    terms = terms.astype(jnp.bfloat16)
    swapped = lax.all_to_all(terms.reshape(dp, rows, 2 * hidden_width), "dp", 0, 0)
    total = jnp.sum(swapped.astype(jnp.float32), axis=0)
    return (gram_loss, total[:, :hidden_width], total[:, hidden_width:], grad_down)


def solution(mesh):
    in_specs = (
        P(("groups", "dp"), None),
        P(("groups", "dp")),
        P(),
        P(),
        P(),
        P(),
        P("groups", "dp"),
        P("dp", None),
        P("groups", None),
        P(),
    )
    out_specs = (
        P("groups"),
        P(("groups", "dp"), None),
        P(("groups", "dp"), None),
        P(("groups", "dp"), None),
    )
    return jax.shard_map(
        per_device, mesh=mesh, in_specs=in_specs, out_specs=out_specs, check_vma=False
    )
```

time: 444 us -> 301 us (0.68)
  the two profiles are of different devices: /device:TPU:0 before, /device:TPU:13 now
where the time goes in v1:
time: 301 us
  waiting for transfers between devices  157 us (52%)
  blocking collectives  63.7 us (21%)
  matrix products  25.1 us (8%)
  starting transfers between devices  19.8 us (7%)
  between operations  16.8 us (6%)
  other arithmetic  15.9 us (5%)
    all_to_all x1, waiting for transfers between devices, per_device(): lax.all_to_all(terms.reshape(dp, rows, 2 * hidden_width), 'dp', 0, 0)  136 us
    psum x1, blocking collectives, per_device(): gram_raw = lax.psum(gram_part, 'dp')  45.7 us
    reduce_scatter x1, waiting for transfers between devices, per_device(): lax.psum_scatter(partial_attn, 'dp', scatter_dimension=1, tiled=True)  20.7 us
    all_to_all x1, starting transfers between devices, per_device(): lax.all_to_all(terms.reshape(dp, rows, 2 * hidden_width), 'dp', 0, 0)  19.8 us
    all_gather x1, blocking collectives, per_device(): packed_all = lax.all_gather(packed, 'dp', axis=0, tiled=True)  18 us
  transfers between devices with their start and end apart: 2, of which 2 were waited for; matrix products, arithmetic and copies ran while one was open for 6% of the time, Pallas kernels for 0%

profile of v1, /device:TPU:13, one launch (start us, length us, event | category | flops | bytes accessed | tf_op | source)
XLA Modules:
  0.0 300.5 jit_solution(8370609172329494020)
XLA Ops:
  7.2 0.0 reduce-scatter.2.cloned.1.call-start
  7.2 3.0 %fusion.35 = f32[32,4096]{1,0:T(8,128)} fusion(bf16[32,256]{1,0:T(8,128)(2,1)} %param.16, bf16[256,4096]{1,0:T(8,128)(2,1)} %param.17), kind=kOutput, calls=%fused_computation.65 | convolution fusion | flops 67108864 | bytes 2637824 | tf_op jit(solution)/shard_map/dot_general | solution.py:39
  10.3 0.0 reduce-scatter.2.cloned.1.call-update
  10.3 0.1 fusion.30
  10.4 1.5 multiply_reduce_fusion.1
  11.9 1.5 multiply_reduce_fusion
  13.5 4.2 %fusion.33 = f32[512,1536]{1,0:T(8,128)S(1)} fusion(bf16[1024,1536]{1,0:T(8,128)(2,1)} %param.13, f32[1024]{0:T(1024)S(1)} %convert_element_type.57, f32[512]{0:T(512)S(1)} %add_rsqrt_fusion, bf16[512,1024]{1,0:T(8,128)(2,1)} %param.10), kind=kOutput, calls=%fused_computation.63 | convolution fusion | flops 1612709888 | bytes 7346176 | tf_op jit(solution)/shard_map/dot_general | solution.py:48
  17.7 3.9 %fusion = (f32[2,1536]{1,0:T(2,128)S(1)}, f32[512,1536]{1,0:T(8,128)}) fusion(f32[2,256]{1,0:T(2,128)S(1)} %get-tuple-element.11, f32[512,1536]{1,0:T(8,128)S(1)} %fusion.33, bf16[1024,1536]{1,0:T(8,128)(2,1)S(1)} %copy-done, f32[1024]{0:T(1024)S(1)} %convert_element_type.57, f32[512]{0:T(512)S(1)} %add_rsqrt_fusion, bf16[512,1024]{1,0:T(8,128)(2,1)S(1)} %copy-done.3), kind=kOutput, calls=%fused_computation.5 | convolution fusion | flops 1619784704 | bytes 10506240 | tf_op jit(solution)/shard_map/dot_general | solution.py:49
  21.6 0.1 broadcast_in_dim.2
  21.6 18.0 %all-gather = f32[16,2,2688]{2,1,0:T(2,128)} all-gather(f32[1,2,2688]{2,1,0:T(2,128)S(1)} %maximum_bitcast_fusion), channel_id=1, replica_groups=mesh['groups'=2,'dp'=16] {'dp'}, dimensions={0}, use_global_device_ids=true | all-gather | bytes 365568 | tf_op jit(solution)/shard_map/all_gather | solution.py:59
  39.6 1.2 reshape.93
  40.9 0.8 dynamic-slice_convert_fusion
  41.7 0.1 slice_reduce_fusion
  41.8 3.7 %multiply_reduce_fusion.3 = (f32[32]{0:T(128)S(1)}, f32[32,1024]{1,0:T(8,128)S(1)}) fusion(f32[32]{0:T(128)S(1)} %slice_reduce_fusion, bf16[1536,1024]{1,0:T(8,128)(2,1)} %param.15, f32[32,2688]{1,0:T(8,128)} %copy-done.5), kind=kOutput, calls=%fused_computation.25 | convolution fusion | flops 604110848 | bytes 3604736 | tf_op jit(solution)/shard_map/dot_general | solution.py:69
  45.5 20.7 %reduce-scatter.2.cloned.1.call-done = f32[32,256]{1,0:T(8,128)} async-done(((f32[32,4096]{1,0:T(8,128)}), f32[32,256]{1,0:T(8,128)}) %reduce-scatter.2.cloned.1.call-update) | async-done | bytes 32784 | tf_op jit(solution)/shard_map/reduce_scatter | solution.py:40
  66.2 1.0 fusion.9
  67.2 45.7 %psum.7 = f32[32,32]{1,0:T(8,128)S(1)} all-reduce(f32[32,32]{1,0:T(8,128)S(1)} %fusion.9), channel_id=1, replica_groups=mesh['groups'=2,'dp'=16] {'dp'}, use_global_device_ids=true, to_apply=%region_5.6 | all-reduce | flops 1024 | bytes 8192 | tf_op jit(solution)/shard_map/psum | solution.py:63
  112.9 0.1 fusion.21
  113.1 0.7 multiply_reduce_fusion.4
  114.4 0.8 multiply_reduce_fusion.5
  116.0 0.4 multiply_reduce_fusion.2
  116.3 0.1 divide_convert_fusion
  116.4 3.0 %fusion.24 = f32[2,1536]{1,0:T(2,128)S(1)} fusion(bf16[1536,1024]{1,0:T(8,128)(2,1)} %param.15, bf16[32,1024]{1,0:T(8,128)(2,1)S(1)} %divide_convert_fusion, s32[]{:T(128)S(6)} %select_n.11), kind=kOutput, calls=%fused_computation.48 | convolution fusion | flops 6291456 | bytes 3162116 | tf_op jit(solution)/shard_map/dot_general | solution.py:17
  119.5 3.5 %fusion.5 = (bf16[512,1536]{1,0:T(8,128)(2,1)S(1)}, bf16[512,1536]{1,0:T(8,128)(2,1)S(1)}) fusion(f32[512,1536]{1,0:T(8,128)} %get-tuple-element.13, f32[512,1536]{1,0:T(8,128)S(1)} %copy-done.2, f32[512]{0:T(512)S(1)} %bitcast.38, f32[2,1536]{1,0:T(2,128)S(1)} %fusion.24), kind=kLoop, calls=%fused_computation.11 | loop fusion | flops 11010048 | bytes 9451520 | tf_op jit(solution)/shard_map/convert_element_type | solution.py:95
  123.0 1.9 convolution_convert_fusion.1
  125.0 1.9 convolution_convert_fusion
  126.9 3.5 %pad_maximum_fusion = bf16[16,64,3072]{2,1,0:T(8,128)(2,1)} fusion(bf16[16,64,1536]{2,1,0:T(8,128)(2,1)S(1)} %bitcast.37, bf16[16,64,1536]{2,1,0:T(8,128)(2,1)S(1)} %bitcast.36), kind=kLoop, calls=%fused_computation.1 | loop fusion | flops 12582912 | bytes 12582912 | tf_op jit(solution)/shard_map/concatenate | solution.py:98
  130.4 19.8 %all-to-all-start = ((bf16[16,64,3072]{2,1,0:T(8,128)(2,1)}), bf16[16,64,3072]{2,1,0:T(8,128)(2,1)}, u32[]{:S(2)}, u32[]{:S(2)}) async-start(bf16[16,64,3072]{2,1,0:T(8,128)(2,1)} %pad_maximum_fusion), calls=%async_computation.1 | async-start | bytes 12582912 | tf_op jit(solution)/shard_map/all_to_all | solution.py:100
  150.2 1.2 fusion.13
  151.4 136.2 %all-to-all-done = bf16[16,64,3072]{2,1,0:T(8,128)(2,1)} async-done(((bf16[16,64,3072]{2,1,0:T(8,128)(2,1)}), bf16[16,64,3072]{2,1,0:T(8,128)(2,1)}, u32[]{:S(2)}, u32[]{:S(2)}) %all-to-all-start) | async-done | bytes 6291488 | tf_op jit(solution)/shard_map/all_to_all | solution.py:100
  287.6 4.0 %convert_reduce_fusion = f32[64,3072]{1,0:T(8,128)S(1)} fusion(bf16[16,64,3072]{2,1,0:T(8,128)(2,1)} %all-to-all-done), kind=kLoop, calls=%fused_computation | loop fusion | flops 6094848 | bytes 7077888 | tf_op jit(solution)/shard_map/reduce_sum | solution.py:101
  291.6 0.9 fusion.34
  (25 shorter events, 0.1 us)
Async XLA Ops:
  7.2 10.5 %copy-start = (bf16[1024,1536]{1,0:T(8,128)(2,1)S(1)}, bf16[1024,1536]{1,0:T(8,128)(2,1)}, u32[]{:S(2)}) copy-start(bf16[1024,1536]{1,0:T(8,128)(2,1)} %param.14) | copy-start | bytes 9437188
  7.2 3.1 %copy-start.7 = (s32[2]{0:T(128)S(1)}, s32[2]{0:T(128)}, u32[]{:S(2)}) copy-start(s32[2]{0:T(128)} %param.11) | copy-start | bytes 28
  7.2 4.7 %copy-start.6 = (bf16[1024]{0:T(1024)(128)(2,1)S(1)}, bf16[1024]{0:T(1024)(128)(2,1)}, u32[]{:S(2)}) copy-start(bf16[1024]{0:T(1024)(128)(2,1)} %param.12) | copy-start | bytes 6148
  7.2 59.0 %reduce-scatter.2.cloned.1.call-start = ((), (), s32[]{:S(2)}) async-start(), calls=%async_computation.2 | async-start | bytes 557056 | tf_op jit(solution)/shard_map/reduce_scatter | solution.py:40
  13.5 4.2 %copy-start.3 = (bf16[512,1024]{1,0:T(8,128)(2,1)S(1)}, bf16[512,1024]{1,0:T(8,128)(2,1)}, u32[]{:S(2)}) copy-start(bf16[512,1024]{1,0:T(8,128)(2,1)} %param.10) | copy-start | bytes 3145732
  17.7 3.9 %copy-start.1 = (f32[512,1536]{1,0:T(8,128)}, f32[512,1536]{1,0:T(8,128)S(1)}, u32[]{:S(2)}) copy-start(f32[512,1536]{1,0:T(8,128)S(1)} %fusion.33) | copy-start | bytes 9437188
  40.9 0.8 copy-start.5
  116.0 3.5 %copy-start.2 = (f32[512,1536]{1,0:T(8,128)S(1)}, f32[512,1536]{1,0:T(8,128)}, u32[]{:S(2)}) copy-start(f32[512,1536]{1,0:T(8,128)} %copy-done.1) | copy-start | bytes 9437188
  119.5 3.5 %copy-start.4 = (bf16[512,1024]{1,0:T(8,128)(2,1)S(1)}, bf16[512,1024]{1,0:T(8,128)(2,1)}, u32[]{:S(2)}) copy-start(bf16[512,1024]{1,0:T(8,128)(2,1)} %param.10) | copy-start | bytes 3145732
  130.4 19.8 %slice-start = ((f32[32,2688]{1,0:T(8,128)}), f32[32,1536]{1,0:T(8,128)S(1)}, s32[]{:S(2)}) async-start(f32[32,2688]{1,0:T(8,128)} %copy-done.5), calls=%async_computation.3 | async-start | bytes 393216 | tf_op jit(solution)/shard_map/slice | solution.py:60
  130.4 157.2 %all-to-all-start = ((bf16[16,64,3072]{2,1,0:T(8,128)(2,1)}), bf16[16,64,3072]{2,1,0:T(8,128)(2,1)}, u32[]{:S(2)}, u32[]{:S(2)}) async-start(bf16[16,64,3072]{2,1,0:T(8,128)(2,1)} %pad_maximum_fusion), calls=%async_computation.1 | async-start | bytes 12582912 | tf_op jit(solution)/shard_map/all_to_all | solution.py:100
Sparse Core Ops, SparseCore 0:
  11.6 54.5 reduce-scatter.1

commit v2 on v0

v2 whole, which is shorter than its diff:
```python
import functools

import jax
import jax.numpy as jnp
from jax import lax
from jax.experimental import pallas as pl
from jax.experimental.pallas import tpu as pltpu
from jax.sharding import PartitionSpec as P

EPS = 1e-06
LOSS_SCALE = 4096.0
MESH = pl.DeviceIdType.MESH
F32 = jnp.float32
BF16 = jnp.bfloat16


def rows_product(left_rows, right_rows):
    return lax.dot_general(
        left_rows, right_rows, (((1,), (1,)), ((), ())), preferred_element_type=F32
    )


def split3(wide):
    high = wide.astype(BF16)
    rest = wide - high.astype(F32)
    middle = rest.astype(BF16)
    low = (rest - middle.astype(F32)).astype(BF16)
    return high, middle, low


def step_kernel(
    n, width,
    states, lengths, norm_gain, w_gate, w_up, w_down, context, w_out, resid, gain,
    loss_out, gate_out, up_out, down_out,
    t_send, t_recv, g_all, p_all, big, feats, feats_in, acts, d_hid,
    y_send, y_part, y_recv, z_send, z_recv, z_part,
    t_ssem, t_rsem, g_ssem, g_rsem, p_ssem, p_rsem, s_ssem, s_rsem,
    y_ssem, y_rsem, z_ssem, z_rsem,
):
    me = lax.axis_index("dp")
    core = lax.rem(me, 2)
    row = lax.rem(lax.div(me, 2), 2)
    col = lax.div(me, 4)
    cols = n // 4
    sibling = me + 1 - 2 * core
    across = me + 2 - 4 * row
    docs_dev = lengths.shape[0]
    tokens, model = states.shape
    seq = tokens // docs_dev
    hidden_width = w_gate.shape[1]
    docs = context.shape[0]
    feat = w_out.shape[1] // n
    rows = model // n
    down_rows = hidden_width // n
    pieces = hidden_width // width
    chunks = 2 * pieces

    def peer(d):
        return lax.rem(me + d, n)

    barrier = pltpu.get_barrier_semaphore()

    @pl.loop(1, n)
    def _(d):
        pl.semaphore_signal(barrier, inc=1, device_id={"dp": peer(d)}, device_id_type=MESH)

    partial = jnp.dot(context[...], w_out[...], preferred_element_type=F32)
    first = (me == 0).astype(F32)
    partial = gain[...].astype(F32) * (partial + first * resid[...].astype(F32))
    for j in range(n):
        t_send[j] = partial[:, j * feat : (j + 1) * feat].astype(BF16)
    t_recv[me] = t_send[me]
    pl.semaphore_wait(barrier, n - 1)

    def t_copy(dst, src):
        return pltpu.make_async_remote_copy(
            src_ref=t_send.at[dst], dst_ref=t_recv.at[src], send_sem=t_ssem.at[dst],
            recv_sem=t_rsem.at[src], device_id={"dp": dst}, device_id_type=MESH,
        )

    @pl.loop(1, n)
    def _(d):
        t_copy(peer(d), me).start()

    normed_parts = []
    masks = []
    for d in range(docs_dev):
        x = states[d * seq : (d + 1) * seq].astype(F32)
        inv_rms = lax.rsqrt(jnp.mean(x * x, axis=1, keepdims=True) + EPS)
        normed_wide = x * inv_rms * norm_gain[...].astype(F32)
        normed = normed_wide.astype(BF16)
        normed_parts.append(normed)
        turned = normed.astype(F32).T.astype(BF16)
        feats[:, :, :, :, d * seq : (d + 1) * seq] = turned.reshape(cols, 2, 2, rows, seq)
        length = lengths[d]
        mask = (lax.broadcasted_iota(jnp.int32, (seq, 1), 0) < length).astype(F32)
        masks.append(mask)
        p_all[me, d : d + 1, hidden_width : hidden_width + model] = jnp.sum(
            x * mask, axis=0, keepdims=True
        )
        p_all[me, d : d + 1, hidden_width + model :] = jnp.zeros((1, 128), F32) + length.astype(F32)
    normed = jnp.concatenate(normed_parts, axis=0)
    mask = jnp.concatenate(masks, axis=0)

    feats_copy = pltpu.make_async_remote_copy(
        src_ref=feats.at[:, :, 1 - core], dst_ref=feats_in, send_sem=s_ssem.at[chunks],
        recv_sem=s_rsem.at[chunks], device_id={"dp": sibling}, device_id_type=MESH,
    )
    feats_copy.start()

    def acts_copy(c):
        return pltpu.make_async_remote_copy(
            src_ref=acts.at[0, c], dst_ref=acts.at[1, c], send_sem=s_ssem.at[c],
            recv_sem=s_rsem.at[c], device_id={"dp": sibling}, device_id_type=MESH,
        )

    @pl.loop(0, pieces)
    def _(c):
        at = pl.ds(pl.multiple_of(c * width, width), width)
        gate_pre = jnp.dot(normed, w_gate[:, at], preferred_element_type=F32)
        up_pre = jnp.dot(normed, w_up[:, at], preferred_element_type=F32)
        sig = jax.nn.sigmoid(gate_pre)
        silu = gate_pre * sig
        hidden = (silu * up_pre).astype(BF16).astype(F32) * mask
        for d in range(docs_dev):
            p_all[me, d : d + 1, at] = jnp.sum(
                hidden[d * seq : (d + 1) * seq], axis=0, keepdims=True
            )
        acts[0, c] = (mask * up_pre * sig * (1.0 + gate_pre * (1.0 - sig))).astype(BF16)
        acts[0, c + pieces] = (mask * silu).astype(BF16)

    def p_copy(dst, src):
        return pltpu.make_async_remote_copy(
            src_ref=p_all.at[src], dst_ref=p_all.at[src], send_sem=p_ssem.at[dst],
            recv_sem=p_rsem.at[src], device_id={"dp": dst}, device_id_type=MESH,
        )

    def g_copy(dst, src):
        return pltpu.make_async_remote_copy(
            src_ref=g_all.at[src], dst_ref=g_all.at[src], send_sem=g_ssem.at[dst],
            recv_sem=g_rsem.at[src], device_id={"dp": dst}, device_id_type=MESH,
        )

    @pl.loop(1, n)
    def _(d):
        p_copy(peer(d), me).start()

    @pl.loop(1, n)
    def _(d):
        t_copy(me, peer(d)).wait_recv()

    scaled = jnp.sum(t_recv[...].astype(F32), axis=0)
    gram_part = lax.dot_general(
        scaled, scaled, (((1,), (1,)), ((), ())), precision=lax.Precision.HIGHEST,
        preferred_element_type=F32,
    )
    fold = max(1, 128 // docs)
    fold_rows = docs // fold
    g_all[me] = jnp.concatenate(
        [gram_part[i * fold_rows : (i + 1) * fold_rows] for i in range(fold)], axis=1
    )

    @pl.loop(1, n)
    def _(d):
        g_copy(peer(d), me).start()

    @pl.loop(0, chunks)
    def _(c):
        acts_copy(c).start()

    @pl.loop(1, n)
    def _(d):
        p_copy(me, peer(d)).wait_recv()

    for j in range(n):
        big[j * docs_dev : (j + 1) * docs_dev, :] = p_all[j]
    sums = jnp.concatenate(split3(big[:, :hidden_width]), axis=0)
    count_all = big[:, hidden_width + model : hidden_width + model + 1]
    lifted = jnp.dot(sums, w_down[...], preferred_element_type=F32)
    lifted = lifted[:docs] + (lifted[docs : 2 * docs] + lifted[2 * docs :])
    pooled = (big[:, hidden_width : hidden_width + model] + lifted) / count_all
    inv_norm = lax.rsqrt(jnp.sum(pooled * pooled, axis=1, keepdims=True) + EPS)
    unit_rows = pooled * inv_norm
    embed = unit_rows.astype(BF16)
    gram_student = rows_product(embed, embed)

    @pl.loop(1, n)
    def _(d):
        g_copy(me, peer(d)).wait_recv()

    folded = jnp.sum(g_all[...], axis=0)
    gram_raw = jnp.concatenate(
        [folded[:, i * docs : (i + 1) * docs] for i in range(fold)], axis=0
    )
    diagonal = lax.broadcasted_iota(jnp.int32, (docs, docs), 0) == lax.broadcasted_iota(
        jnp.int32, (docs, docs), 1
    )
    squares = jnp.where(diagonal, gram_raw, 0.0)
    inv_col = lax.rsqrt(jnp.sum(squares, axis=1, keepdims=True) + EPS)
    inv_row = lax.rsqrt(jnp.sum(squares, axis=0, keepdims=True) + EPS)
    gram_teacher = gram_raw * inv_col * inv_row
    gram_diff = gram_student - gram_teacher

    def total(square):
        return jnp.sum(jnp.sum(square, axis=1, keepdims=True), axis=0, keepdims=True)

    diff_norm = jnp.sqrt(total(gram_diff * gram_diff) + EPS)
    teacher_norm = jnp.sqrt(total(gram_teacher * gram_teacher))
    loss_out[...] = diff_norm / teacher_norm
    d_gram = LOSS_SCALE * gram_diff / (diff_norm * teacher_norm)
    spread = jnp.dot(
        jnp.concatenate(split3(d_gram), axis=0), embed, preferred_element_type=F32
    )
    d_embed = 2.0 * (spread[:docs] + (spread[docs : 2 * docs] + spread[2 * docs :]))
    along = jnp.sum(unit_rows * d_embed, axis=1, keepdims=True)
    d_all = ((d_embed - unit_rows * along) * inv_norm / count_all).astype(BF16)

    pick = lax.broadcasted_iota(jnp.int32, (16, docs), 0)
    wanted = jnp.where(
        pick < docs_dev, me * docs_dev + pick, sibling * docs_dev + pick - docs_dev
    )
    chosen = (wanted == lax.broadcasted_iota(jnp.int32, (16, docs), 1)).astype(F32).astype(BF16)
    d_pair = jnp.dot(chosen, d_all, preferred_element_type=F32).astype(BF16)
    d_pair_hidden = rows_product(d_pair, w_down[...])
    for c in range(chunks):
        at = (c % pieces) * width
        d_hid[c] = d_pair_hidden[:, at : at + width]

    feats_copy.wait_recv()

    def y_copy(c):
        return pltpu.make_async_remote_copy(
            src_ref=y_send.at[c], dst_ref=y_recv.at[c], send_sem=y_ssem.at[c],
            recv_sem=y_rsem.at[c], device_id={"dp": across}, device_id_type=MESH,
        )

    def z_copy(c, there, src):
        return pltpu.make_async_remote_copy(
            src_ref=z_send.at[c, there], dst_ref=z_recv.at[c, src],
            send_sem=z_ssem.at[c, there], recv_sem=z_rsem.at[c, src],
            device_id={"dp": there * 4 + row * 2 + core}, device_id_type=MESH,
        )

    def col_peer(d):
        return lax.rem(col + d, cols)

    @pl.loop(0, chunks)
    def _(c):
        acts_copy(c).wait_recv()
        d_mine, d_other = [], []
        for d in range(docs_dev):
            token_at = slice(d * seq, (d + 1) * seq)
            mine = d_hid[c, d : d + 1]
            other = d_hid[c, docs_dev + d : docs_dev + d + 1]
            d_mine.append((acts[0, c, token_at].astype(F32) * mine).astype(BF16))
            d_other.append((acts[1, c, token_at].astype(F32) * other).astype(BF16))
        d_mine = jnp.concatenate(d_mine, axis=0)
        d_other = jnp.concatenate(d_other, axis=0)

        def term(side):
            own = feats[:, side, core].reshape(cols * rows, tokens)
            given = feats_in[:, side].reshape(cols * rows, tokens)
            both = jnp.dot(own, d_mine, preferred_element_type=F32) + jnp.dot(
                given, d_other, preferred_element_type=F32
            )
            return both.reshape(cols, rows, width)

        y_send[c] = term(1 - row).astype(BF16)
        y_copy(c).start()
        y_part[c] = term(row)

    own_rows = lax.broadcasted_iota(jnp.int32, (down_rows, hidden_width), 0) + me * down_rows
    select = (
        own_rows == lax.broadcasted_iota(jnp.int32, (down_rows, hidden_width), 1)
    ).astype(F32).astype(BF16)
    own_sums = rows_product(select, sums).astype(BF16)
    down_out[...] = jnp.dot(
        own_sums, jnp.concatenate([d_all] * 3, axis=0), preferred_element_type=F32
    )

    @pl.loop(0, chunks)
    def _(c):
        y_copy(c).wait_recv()
        both = y_part[c] + y_recv[c].astype(F32)
        y_part[c] = both
        z_send[c] = both.astype(BF16)
        z_part[c] = y_part[c, col]

        @pl.loop(1, cols)
        def _(d):
            z_copy(c, col_peer(d), col).start()

    @pl.loop(0, chunks)
    def _(c):
        @pl.loop(1, cols)
        def _(d):
            z_copy(c, col, col_peer(d)).wait_recv()
            z_part[c] += z_recv[c, col_peer(d)].astype(F32)

    for c in range(pieces):
        gate_out[:, c * width : (c + 1) * width] = z_part[c]
        up_out[:, c * width : (c + 1) * width] = z_part[c + pieces]

    feats_copy.wait_send()

    @pl.loop(1, n)
    def _(d):
        t_copy(peer(d), me).wait_send()
        p_copy(peer(d), me).wait_send()
        g_copy(peer(d), me).wait_send()

    @pl.loop(0, chunks)
    def _(c):
        acts_copy(c).wait_send()
        y_copy(c).wait_send()

        @pl.loop(1, cols)
        def _(d):
            z_copy(c, col_peer(d), col).wait_send()


def solution(mesh):
    n = mesh.shape["dp"]
    in_specs = (
        P(("groups", "dp"), None),
        P(("groups", "dp")),
        P(),
        P(),
        P(),
        P(),
        P("groups", "dp"),
        P("dp", None),
        P("groups", None),
        P(),
    )
    out_specs = (
        P("groups"),
        P(("groups", "dp"), None),
        P(("groups", "dp"), None),
        P(("groups", "dp"), None),
    )

    def per_device(
        states, lengths, norm_gain, w_gate, w_up, w_down, context, w_out, resid_stream, teacher_gain
    ):
        tokens, model = states.shape
        hidden_width = w_gate.shape[1]
        docs_dev = lengths.shape[0]
        docs = context.shape[0]
        teacher_width = w_out.shape[1]
        feat = teacher_width // n
        rows = model // n
        width = 512
        chunks = 2 * hidden_width // width
        cols = n // 4
        fold = max(1, 128 // docs)
        packed = hidden_width + model + 128
        vmem = pl.BlockSpec(memory_space=pltpu.VMEM)
        sem = pltpu.SemaphoreType.DMA
        loss, grad_gate, grad_up, grad_down = pl.pallas_call(
            functools.partial(step_kernel, n, width),
            out_shape=(
                jax.ShapeDtypeStruct((1, 1), F32),
                jax.ShapeDtypeStruct((rows, hidden_width), F32),
                jax.ShapeDtypeStruct((rows, hidden_width), F32),
                jax.ShapeDtypeStruct((hidden_width // n, model), F32),
            ),
            in_specs=[vmem, pl.BlockSpec(memory_space=pltpu.SMEM)] + [vmem] * 8,
            out_specs=(vmem,) * 4,
            scratch_shapes=[
                pltpu.VMEM((n, docs, feat), BF16),
                pltpu.VMEM((n, docs, feat), BF16),
                pltpu.VMEM((n, docs // fold, docs * fold), F32),
                pltpu.VMEM((n, docs_dev, packed), F32),
                pltpu.VMEM((docs, packed), F32),
                pltpu.VMEM((cols, 2, 2, rows, tokens), BF16),
                pltpu.VMEM((cols, 2, rows, tokens), BF16),
                pltpu.VMEM((2, chunks, tokens, width), BF16),
                pltpu.VMEM((chunks, 16, width), F32),
                pltpu.VMEM((chunks, cols, rows, width), BF16),
                pltpu.VMEM((chunks, cols, rows, width), F32),
                pltpu.VMEM((chunks, cols, rows, width), BF16),
                pltpu.VMEM((chunks, cols, rows, width), BF16),
                pltpu.VMEM((chunks, cols, rows, width), BF16),
                pltpu.VMEM((chunks, rows, width), F32),
                sem((n,)), sem((n,)), sem((n,)), sem((n,)), sem((n,)), sem((n,)),
                sem((chunks + 1,)), sem((chunks + 1,)),
                sem((chunks,)), sem((chunks,)),
                sem((chunks, cols)), sem((chunks, cols)),
            ],
            compiler_params=pltpu.CompilerParams(
                collective_id=0, has_side_effects=True, vmem_limit_bytes=60 * 1024 * 1024
            ),
        )(
            states, lengths, norm_gain.reshape(1, -1), w_gate, w_up, w_down, context, w_out,
            resid_stream, teacher_gain.reshape(1, -1),
        )
        return (loss.reshape(1), grad_gate, grad_up, grad_down)

    return jax.shard_map(
        per_device, mesh=mesh, in_specs=in_specs, out_specs=out_specs, check_vma=False
    )
```

time: 444 us -> 85.2 us (0.19)
  waiting for transfers between devices: 306 us -> 0 us
  blocking collectives: 75.3 us -> 0 us
  Pallas kernels: 0 us -> 74.6 us
  matrix products: 35.5 us -> 0 us
  between operations: 17.2 us -> 2.39 us
  other arithmetic: 7.69 us -> 0 us
  local copies, waits for them, and re-layouts: 1.47 us -> 7.89 us
    reduce_scatter x3 -> x0, waiting for transfers between devices: 248 us -> none  [the longest x1 89.6 us: per_device(): lax.psum_scatter(term_up, 'dp', scatter_dimension=0, tiled=True)]
    pallas_call x0 -> x1, Pallas kernels: none -> 74.6 us  [per_device(): pl.pallas_call(functools.partial(step_kernel, n, width), out_shape=(jax.S...]
    unnamed x5 -> x0, waiting for transfers between devices: 57.7 us -> none
    all_gather x2 -> x0, blocking collectives: 44.8 us -> none  [the longest x1 23.3 us: per_device(): embed_all = lax.all_gather(embed_own, 'dp', axis=0, tiled=True)]
    dot_general x11 -> x0, matrix products: 35.5 us -> none  [the longest x3 16.9 us: cols_product(): lax.dot_general(left_cols, right_cols, (((0,), (0,)), ((), ())), preferre...]
    psum x1 -> x0, blocking collectives: 30.4 us -> none  [per_device(): total_diff, total_teacher = lax.psum((diff_square, teacher_square), 'dp')]
    convert_element_type x6 -> x0, other arithmetic: 4.67 us -> none  [the longest x1 4.4 us: per_device(): d_up = (d_hidden_tok * jax.nn.silu(gate_pre)).astype(jnp.bfloat16)]
  transfers between devices with their start and end apart: 4 -> 0, of which waited for: 4 -> 0; matrix products, arithmetic and copies ran while one was open for 6% -> 0% of each run, Pallas kernels for 0% -> 0%
where the time goes in v2:
time: 85.2 us; the launch traced here: 84.9 us
  Pallas kernels  74.6 us (88%)
  local copies, waits for them, and re-layouts  7.89 us (9%)
  between operations  2.39 us (3%)
    pallas_call x1, Pallas kernels, per_device(): pl.pallas_call(functools.partial(step_kernel, n, width), out_shape=(jax.S...  74.6 us
    unnamed x3, local copies, waits for them, and re-layouts  5.3 us

profile of v2, /device:TPU:0, one launch (start us, length us, event | category | flops | bytes accessed | tf_op | source)
XLA Modules:
  0.0 84.9 jit_solution(4983754324550457402)
XLA Ops:
  0.6 1.3 %reshape.17.norm_gain = bf16[1,1024]{1,0:T(2,128)(2,1)} reshape(bf16[1024]{0:T(1024)(128)(2,1)} %param.12) | data formatting | bytes 4096 | tf_op jit(solution)/shard_map/reshape | solution.py:395
  1.9 1.3 %reshape.18.gain = bf16[1,4096]{1,0:T(2,128)(2,1)} reshape(bf16[4096]{0:T(1024)(128)(2,1)} %param.19) | data formatting | bytes 16384 | tf_op jit(solution)/shard_map/reshape | solution.py:396
  3.2 74.6 %shard_map.129 = (f32[1,1]{1,0:T(1,128)}, f32[64,1536]{1,0:T(8,128)}, f32[64,1536]{1,0:T(8,128)}, f32[96,1024]{1,0:T(8,128)}) custom-call(bf16[512,1024]{1,0:T(8,128)(2,1)} %states.1, s32[2]{0:T(128)} %lengths.1, bf16[1,1024]{1,0:T(2,128)(2,1)} %reshape.17.norm_gain, bf16[1024,1536]{1,0:T(8,128)(2,1)} %w_gate.1, bf16[1024,1536]{1,0:T(8,128)(2,1)} %w_up.1, ...), custom_call_target="tpu_custom_call" | custom-call | tf_op jit(solution)/shard_map/pallas_call | solution.py:360
  78.5 1.8 %copy.19 = f32[64,1536]{1,0:T(8,128)} copy(f32[64,1536]{1,0:T(8,128)} %get-tuple-element.17) | data formatting | bytes 786432
  80.2 1.8 %copy.20 = f32[64,1536]{1,0:T(8,128)} copy(f32[64,1536]{1,0:T(8,128)} %get-tuple-element.18) | data formatting | bytes 786432
  82.0 1.8 %copy.21 = f32[96,1024]{1,0:T(8,128)} copy(f32[96,1024]{1,0:T(8,128)} %get-tuple-element.19) | data formatting | bytes 786432

commit v3 on v2

--- a/solution.py
+++ b/solution.py
@@ -30,11 +30,12 @@
 
 def step_kernel(
     n, width,
-    states, lengths, norm_gain, w_gate, w_up, w_down, context, w_out, resid, gain,
+    states_in, lengths, norm_gain, w_gate_in, w_up_in, w_down_in, context_in, w_out_in, resid_in, gain,
     loss_out, gate_out, up_out, down_out,
-    t_send, t_recv, g_all, p_all, big, feats, feats_in, acts, d_hid,
+    states, w_gate, w_up, w_down, context, w_out, resid,
+    t_send, t_recv, g_all, p_all, h_all, s_own, big, big_h, feats, feats_in, acts, d_hid,
     y_send, y_part, y_recv, z_send, z_recv, z_part,
-    t_ssem, t_rsem, g_ssem, g_rsem, p_ssem, p_rsem, s_ssem, s_rsem,
+    in_sem, wide_sem, t_ssem, t_rsem, g_ssem, g_rsem, p_ssem, p_rsem, h_ssem, h_rsem, s_ssem, s_rsem,
     y_ssem, y_rsem, z_ssem, z_rsem,
 ):
     me = lax.axis_index("dp")
@@ -58,15 +59,39 @@
     def peer(d):
         return lax.rem(me + d, n)
 
+    def load(i, src, dst):
+        copy = pltpu.make_async_copy(src, dst, in_sem.at[i])
+        copy.start()
+        return copy
+
+    def load_wide(c):
+        at = pl.ds(pl.multiple_of(c * width, width), width)
+        return (
+            pltpu.make_async_copy(w_gate_in.at[:, at], w_gate.at[:, at], wide_sem.at[0, c]),
+            pltpu.make_async_copy(w_up_in.at[:, at], w_up.at[:, at], wide_sem.at[1, c]),
+        )
+
+    context_load = load(0, context_in, context)
+    w_out_load = load(1, w_out_in, w_out)
+    resid_load = load(2, resid_in, resid)
+    states_load = load(3, states_in, states)
+    for c in range(pieces):
+        for copy in load_wide(c):
+            copy.start()
+    w_down_load = load(4, w_down_in, w_down)
+
     barrier = pltpu.get_barrier_semaphore()
 
     @pl.loop(1, n)
     def _(d):
         pl.semaphore_signal(barrier, inc=1, device_id={"dp": peer(d)}, device_id_type=MESH)
 
+    context_load.wait()
+    w_out_load.wait()
+    resid_load.wait()
     partial = jnp.dot(context[...], w_out[...], preferred_element_type=F32)
     first = (me == 0).astype(F32)
-    partial = gain[...].astype(F32) * (partial + first * resid[...].astype(F32))
+    partial = gain[...].astype(F32).reshape(1, -1) * (partial + first * resid[...].astype(F32))
     for j in range(n):
         t_send[j] = partial[:, j * feat : (j + 1) * feat].astype(BF16)
     t_recv[me] = t_send[me]
@@ -82,12 +107,13 @@
     def _(d):
         t_copy(peer(d), me).start()
 
+    states_load.wait()
     normed_parts = []
     masks = []
     for d in range(docs_dev):
         x = states[d * seq : (d + 1) * seq].astype(F32)
         inv_rms = lax.rsqrt(jnp.mean(x * x, axis=1, keepdims=True) + EPS)
-        normed_wide = x * inv_rms * norm_gain[...].astype(F32)
+        normed_wide = x * inv_rms * norm_gain[...].astype(F32).reshape(1, -1)
         normed = normed_wide.astype(BF16)
         normed_parts.append(normed)
         turned = normed.astype(F32).T.astype(BF16)
@@ -95,10 +121,8 @@
         length = lengths[d]
         mask = (lax.broadcasted_iota(jnp.int32, (seq, 1), 0) < length).astype(F32)
         masks.append(mask)
-        p_all[me, d : d + 1, hidden_width : hidden_width + model] = jnp.sum(
-            x * mask, axis=0, keepdims=True
-        )
-        p_all[me, d : d + 1, hidden_width + model :] = jnp.zeros((1, 128), F32) + length.astype(F32)
+        s_own[d : d + 1] = jnp.sum(x * mask, axis=0, keepdims=True)
+        p_all[me, d : d + 1, model:] = jnp.zeros((1, 128), F32) + length.astype(F32)
     normed = jnp.concatenate(normed_parts, axis=0)
     mask = jnp.concatenate(masks, axis=0)
 
@@ -117,13 +141,15 @@
     @pl.loop(0, pieces)
     def _(c):
         at = pl.ds(pl.multiple_of(c * width, width), width)
+        for copy in load_wide(c):
+            copy.wait()
         gate_pre = jnp.dot(normed, w_gate[:, at], preferred_element_type=F32)
         up_pre = jnp.dot(normed, w_up[:, at], preferred_element_type=F32)
         sig = jax.nn.sigmoid(gate_pre)
         silu = gate_pre * sig
         hidden = (silu * up_pre).astype(BF16).astype(F32) * mask
         for d in range(docs_dev):
-            p_all[me, d : d + 1, at] = jnp.sum(
+            h_all[me, d : d + 1, at] = jnp.sum(
                 hidden[d * seq : (d + 1) * seq], axis=0, keepdims=True
             )
         acts[0, c] = (mask * up_pre * sig * (1.0 + gate_pre * (1.0 - sig))).astype(BF16)
@@ -135,11 +161,23 @@
             recv_sem=p_rsem.at[src], device_id={"dp": dst}, device_id_type=MESH,
         )
 
+    def h_copy(dst, src):
+        return pltpu.make_async_remote_copy(
+            src_ref=h_all.at[src], dst_ref=h_all.at[src], send_sem=h_ssem.at[dst],
+            recv_sem=h_rsem.at[src], device_id={"dp": dst}, device_id_type=MESH,
+        )
+
     def g_copy(dst, src):
         return pltpu.make_async_remote_copy(
             src_ref=g_all.at[src], dst_ref=g_all.at[src], send_sem=g_ssem.at[dst],
             recv_sem=g_rsem.at[src], device_id={"dp": dst}, device_id_type=MESH,
         )
+
+    w_down_load.wait()
+    own_parts = jnp.concatenate([part.astype(F32) for part in split3(h_all[me])], axis=0)
+    lifted = jnp.dot(own_parts.astype(BF16), w_down[...], preferred_element_type=F32)
+    lifted = lifted[:docs_dev] + (lifted[docs_dev : 2 * docs_dev] + lifted[2 * docs_dev :])
+    p_all[me, :, :model] = (s_own[...] + lifted) / p_all[me, :, model : model + 1]
 
     @pl.loop(1, n)
     def _(d):
@@ -164,6 +202,10 @@
     def _(d):
         g_copy(peer(d), me).start()
 
+    @pl.loop(1, n)
+    def _(d):
+        h_copy(peer(d), me).start()
+
     @pl.loop(0, chunks)
     def _(c):
         acts_copy(c).start()
@@ -174,11 +216,8 @@
 
     for j in range(n):
         big[j * docs_dev : (j + 1) * docs_dev, :] = p_all[j]
-    sums = jnp.concatenate(split3(big[:, :hidden_width]), axis=0)
-    count_all = big[:, hidden_width + model : hidden_width + model + 1]
-    lifted = jnp.dot(sums, w_down[...], preferred_element_type=F32)
-    lifted = lifted[:docs] + (lifted[docs : 2 * docs] + lifted[2 * docs :])
-    pooled = (big[:, hidden_width : hidden_width + model] + lifted) / count_all
+    count_all = big[:, model : model + 1]
+    pooled = big[:, :model]
     inv_norm = lax.rsqrt(jnp.sum(pooled * pooled, axis=1, keepdims=True) + EPS)
     unit_rows = pooled * inv_norm
     embed = unit_rows.astype(BF16)
@@ -269,6 +308,13 @@
         y_copy(c).start()
         y_part[c] = term(row)
 
+    @pl.loop(1, n)
+    def _(d):
+        h_copy(me, peer(d)).wait_recv()
+
+    for j in range(n):
+        big_h[j * docs_dev : (j + 1) * docs_dev, :] = h_all[j]
+    sums = jnp.concatenate(split3(big_h[...]), axis=0)
     own_rows = lax.broadcasted_iota(jnp.int32, (down_rows, hidden_width), 0) + me * down_rows
     select = (
         own_rows == lax.broadcasted_iota(jnp.int32, (down_rows, hidden_width), 1)
@@ -308,6 +354,7 @@
         t_copy(peer(d), me).wait_send()
         p_copy(peer(d), me).wait_send()
         g_copy(peer(d), me).wait_send()
+        h_copy(peer(d), me).wait_send()
 
     @pl.loop(0, chunks)
     def _(c):
@@ -317,6 +364,12 @@
         @pl.loop(1, cols)
         def _(d):
             z_copy(c, col_peer(d), col).wait_send()
+
+
+def hand_over(gate, up, down, gate_out, up_out, down_out):
+    gate_out[...] = gate[...]
+    up_out[...] = up[...]
+    down_out[...] = down[...]
 
 
 def solution(mesh):
@@ -350,11 +403,12 @@
         teacher_width = w_out.shape[1]
         feat = teacher_width // n
         rows = model // n
-        width = 512
+        width = 256
         chunks = 2 * hidden_width // width
         cols = n // 4
         fold = max(1, 128 // docs)
-        packed = hidden_width + model + 128
+        packed = model + 128
+        hbm = pl.BlockSpec(memory_space=pl.ANY)
         vmem = pl.BlockSpec(memory_space=pltpu.VMEM)
         sem = pltpu.SemaphoreType.DMA
         loss, grad_gate, grad_up, grad_down = pl.pallas_call(
@@ -365,14 +419,24 @@
                 jax.ShapeDtypeStruct((rows, hidden_width), F32),
                 jax.ShapeDtypeStruct((hidden_width // n, model), F32),
             ),
-            in_specs=[vmem, pl.BlockSpec(memory_space=pltpu.SMEM)] + [vmem] * 8,
+            in_specs=[hbm, pl.BlockSpec(memory_space=pltpu.SMEM), vmem] + [hbm] * 6 + [vmem],
             out_specs=(vmem,) * 4,
             scratch_shapes=[
+                pltpu.VMEM((tokens, model), BF16),
+                pltpu.VMEM((model, hidden_width), BF16),
+                pltpu.VMEM((model, hidden_width), BF16),
+                pltpu.VMEM((hidden_width, model), BF16),
+                pltpu.VMEM(context.shape, BF16),
+                pltpu.VMEM(w_out.shape, BF16),
+                pltpu.VMEM(resid_stream.shape, BF16),
                 pltpu.VMEM((n, docs, feat), BF16),
                 pltpu.VMEM((n, docs, feat), BF16),
                 pltpu.VMEM((n, docs // fold, docs * fold), F32),
                 pltpu.VMEM((n, docs_dev, packed), F32),
+                pltpu.VMEM((n, docs_dev, hidden_width), F32),
+                pltpu.VMEM((docs_dev, model), F32),
                 pltpu.VMEM((docs, packed), F32),
+                pltpu.VMEM((docs, hidden_width), F32),
                 pltpu.VMEM((cols, 2, 2, rows, tokens), BF16),
                 pltpu.VMEM((cols, 2, rows, tokens), BF16),
                 pltpu.VMEM((2, chunks, tokens, width), BF16),
@@ -383,7 +447,8 @@
                 pltpu.VMEM((chunks, cols, rows, width), BF16),
                 pltpu.VMEM((chunks, cols, rows, width), BF16),
                 pltpu.VMEM((chunks, rows, width), F32),
-                sem((n,)), sem((n,)), sem((n,)), sem((n,)), sem((n,)), sem((n,)),
+                sem((5,)), sem((2, chunks // 2)),
+                sem((n,)), sem((n,)), sem((n,)), sem((n,)), sem((n,)), sem((n,)), sem((n,)), sem((n,)),
                 sem((chunks + 1,)), sem((chunks + 1,)),
                 sem((chunks,)), sem((chunks,)),
                 sem((chunks, cols)), sem((chunks, cols)),
@@ -392,10 +457,17 @@
                 collective_id=0, has_side_effects=True, vmem_limit_bytes=60 * 1024 * 1024
             ),
         )(
-            states, lengths, norm_gain.reshape(1, -1), w_gate, w_up, w_down, context, w_out,
-            resid_stream, teacher_gain.reshape(1, -1),
-        )
-        return (loss.reshape(1), grad_gate, grad_up, grad_down)
+            states, lengths, norm_gain, w_gate, w_up, w_down, context, w_out,
+            resid_stream, teacher_gain,
+        )
+        made = (grad_gate, grad_up, grad_down)
+        made = pl.pallas_call(
+            hand_over,
+            out_shape=tuple(jax.ShapeDtypeStruct(g.shape, g.dtype) for g in made),
+            in_specs=[vmem] * 3,
+            out_specs=(vmem,) * 3,
+        )(*made)
+        return (loss.reshape(1), *made)
 
     return jax.shard_map(
         per_device, mesh=mesh, in_specs=in_specs, out_specs=out_specs, check_vma=False

time: 85.2 us -> 77.8 us (0.913)
  local copies, waits for them, and re-layouts: 7.89 us -> 0 us
    unnamed x3 -> x0, local copies, waits for them, and re-layouts: 5.3 us -> none
    reshape x2 -> x0, local copies, waits for them, and re-layouts: 2.59 us -> none  [the longest x1 1.31 us: per_device(): teacher_gain.reshape(1, -1)]
    pallas_call x0 -> x1, Pallas kernels: none -> 2.27 us  [per_device(): pl.pallas_call(hand_over, out_shape=tuple((jax.ShapeDtypeStruct(g.shape,...]
    pallas_call x1, Pallas kernels: 74.6 us -> 72.9 us  [per_device(): pl.pallas_call(functools.partial(step_kernel, n, width), out_shape=(jax.S...]
where the time goes in v3:
time: 77.8 us; the launch traced here: 77.6 us
  Pallas kernels  75.2 us (97%)
  between operations  2.38 us (3%)
    pallas_call x1, Pallas kernels, per_device(): pl.pallas_call(functools.partial(step_kernel, n, width), out_shape=(jax.S...  72.9 us
    pallas_call x1, Pallas kernels, per_device(): pl.pallas_call(hand_over, out_shape=tuple((jax.ShapeDtypeStruct(g.shape,...  2.27 us

profile of v3, /device:TPU:0, one launch (start us, length us, event | category | flops | bytes accessed | tf_op | source)
XLA Modules:
  0.0 77.6 jit_solution(3673393355534989620)
XLA Ops:
  0.6 72.9 %shard_map.129 = (f32[1,1]{1,0:T(1,128)}, f32[64,1536]{1,0:T(8,128)}, f32[64,1536]{1,0:T(8,128)}, f32[96,1024]{1,0:T(8,128)}) custom-call(bf16[512,1024]{1,0:T(8,128)(2,1)} %states_in.1, s32[2]{0:T(128)} %lengths.1, bf16[1024]{0:T(1024)(128)(2,1)} %norm_gain.1, bf16[1024,1536]{1,0:T(8,128)(2,1)} %w_gate_in.1, bf16[1024,1536]{1,0:T(8,128)(2,1)} %w_up_in.1, ...), custom_call_target="tpu_custom_call" | custom-call | tf_op jit(solution)/shard_map/pallas_call | solution.py:414
  73.6 2.3 %shard_map.130 = (f32[64,1536]{1,0:T(8,128)}, f32[64,1536]{1,0:T(8,128)}, f32[96,1024]{1,0:T(8,128)}) custom-call(f32[64,1536]{1,0:T(8,128)} %get-tuple-element.12.gate, f32[64,1536]{1,0:T(8,128)} %get-tuple-element.13.up, f32[96,1024]{1,0:T(8,128)} %get-tuple-element.14.down), custom_call_target="tpu_custom_call" | custom-call | tf_op jit(solution)/shard_map/pallas_call | solution.py:464

commit v4 on v3

--- a/solution.py
+++ b/solution.py
@@ -34,9 +34,9 @@
     loss_out, gate_out, up_out, down_out,
     states, w_gate, w_up, w_down, context, w_out, resid,
     t_send, t_recv, g_all, p_all, h_all, s_own, big, big_h, feats, feats_in, acts, d_hid,
-    y_send, y_part, y_recv, z_send, z_recv, z_part,
+    y_send, y_part, y_recv, n_send, n_recv, z_send, z_recv, z_part,
     in_sem, wide_sem, t_ssem, t_rsem, g_ssem, g_rsem, p_ssem, p_rsem, h_ssem, h_rsem, s_ssem, s_rsem,
-    y_ssem, y_rsem, z_ssem, z_rsem,
+    y_ssem, y_rsem, n_ssem, n_rsem, z_ssem, z_rsem,
 ):
     me = lax.axis_index("dp")
     core = lax.rem(me, 2)
@@ -273,15 +273,27 @@
             recv_sem=y_rsem.at[c], device_id={"dp": across}, device_id_type=MESH,
         )
 
+    parity = lax.rem(col, 2)
+    half = lax.div(col, 2)
+    halves = cols // 2
+    lane = row * 2 + core
+
+    def n_copy(c):
+        return pltpu.make_async_remote_copy(
+            src_ref=n_send.at[c], dst_ref=n_recv.at[c], send_sem=n_ssem.at[c],
+            recv_sem=n_rsem.at[c], device_id={"dp": (col + 1 - 2 * parity) * 4 + lane},
+            device_id_type=MESH,
+        )
+
     def z_copy(c, there, src):
         return pltpu.make_async_remote_copy(
             src_ref=z_send.at[c, there], dst_ref=z_recv.at[c, src],
             send_sem=z_ssem.at[c, there], recv_sem=z_rsem.at[c, src],
-            device_id={"dp": there * 4 + row * 2 + core}, device_id_type=MESH,
-        )
-
-    def col_peer(d):
-        return lax.rem(col + d, cols)
+            device_id={"dp": (there * 2 + parity) * 4 + lane}, device_id_type=MESH,
+        )
+
+    def half_peer(d):
+        return lax.rem(half + d, halves)
 
     @pl.loop(0, chunks)
     def _(c):
@@ -302,7 +314,7 @@
             both = jnp.dot(own, d_mine, preferred_element_type=F32) + jnp.dot(
                 given, d_other, preferred_element_type=F32
             )
-            return both.reshape(cols, rows, width)
+            return both.reshape(cols // 2, 2, rows, width)
 
         y_send[c] = term(1 - row).astype(BF16)
         y_copy(c).start()
@@ -324,24 +336,34 @@
         own_sums, jnp.concatenate([d_all] * 3, axis=0), preferred_element_type=F32
     )
 
+    def far(c):
+        n_copy(c).wait_recv()
+        z_send[c] = (y_part[c, :, parity] + n_recv[c].astype(F32)).astype(BF16)
+        z_part[c] = y_part[c, half, parity] + n_recv[c, half].astype(F32)
+
+        @pl.loop(1, halves)
+        def _(d):
+            z_copy(c, half_peer(d), half).start()
+
     @pl.loop(0, chunks)
     def _(c):
         y_copy(c).wait_recv()
-        both = y_part[c] + y_recv[c].astype(F32)
-        y_part[c] = both
-        z_send[c] = both.astype(BF16)
-        z_part[c] = y_part[c, col]
-
-        @pl.loop(1, cols)
+        y_part[c] += y_recv[c].astype(F32)
+        n_send[c] = y_part[c, :, 1 - parity].astype(BF16)
+        n_copy(c).start()
+
+        @pl.when(c > 0)
+        def _():
+            far(c - 1)
+
+    far(chunks - 1)
+
+    @pl.loop(0, chunks)
+    def _(c):
+        @pl.loop(1, halves)
         def _(d):
-            z_copy(c, col_peer(d), col).start()
-
-    @pl.loop(0, chunks)
-    def _(c):
-        @pl.loop(1, cols)
-        def _(d):
-            z_copy(c, col, col_peer(d)).wait_recv()
-            z_part[c] += z_recv[c, col_peer(d)].astype(F32)
+            z_copy(c, half, half_peer(d)).wait_recv()
+            z_part[c] += z_recv[c, half_peer(d)].astype(F32)
 
     for c in range(pieces):
         gate_out[:, c * width : (c + 1) * width] = z_part[c]
@@ -360,10 +382,11 @@
     def _(c):
         acts_copy(c).wait_send()
         y_copy(c).wait_send()
-
-        @pl.loop(1, cols)
+        n_copy(c).wait_send()
+
+        @pl.loop(1, halves)
         def _(d):
-            z_copy(c, col_peer(d), col).wait_send()
+            z_copy(c, half_peer(d), half).wait_send()
 
 
 def hand_over(gate, up, down, gate_out, up_out, down_out):
@@ -441,17 +464,19 @@
                 pltpu.VMEM((cols, 2, rows, tokens), BF16),
                 pltpu.VMEM((2, chunks, tokens, width), BF16),
                 pltpu.VMEM((chunks, 16, width), F32),
-                pltpu.VMEM((chunks, cols, rows, width), BF16),
-                pltpu.VMEM((chunks, cols, rows, width), F32),
-                pltpu.VMEM((chunks, cols, rows, width), BF16),
-                pltpu.VMEM((chunks, cols, rows, width), BF16),
-                pltpu.VMEM((chunks, cols, rows, width), BF16),
+                pltpu.VMEM((chunks, cols // 2, 2, rows, width), BF16),
+                pltpu.VMEM((chunks, cols // 2, 2, rows, width), F32),
+                pltpu.VMEM((chunks, cols // 2, 2, rows, width), BF16),
+                pltpu.VMEM((chunks, cols // 2, rows, width), BF16),
+                pltpu.VMEM((chunks, cols // 2, rows, width), BF16),
+                pltpu.VMEM((chunks, cols // 2, rows, width), BF16),
+                pltpu.VMEM((chunks, cols // 2, rows, width), BF16),
                 pltpu.VMEM((chunks, rows, width), F32),
                 sem((5,)), sem((2, chunks // 2)),
                 sem((n,)), sem((n,)), sem((n,)), sem((n,)), sem((n,)), sem((n,)), sem((n,)), sem((n,)),
                 sem((chunks + 1,)), sem((chunks + 1,)),
-                sem((chunks,)), sem((chunks,)),
-                sem((chunks, cols)), sem((chunks, cols)),
+                sem((chunks,)), sem((chunks,)), sem((chunks,)), sem((chunks,)),
+                sem((chunks, cols // 2)), sem((chunks, cols // 2)),
             ],
             compiler_params=pltpu.CompilerParams(
                 collective_id=0, has_side_effects=True, vmem_limit_bytes=60 * 1024 * 1024

time: 77.8 us -> 76.1 us (0.978)
  Pallas kernels: 75.2 us -> 73.4 us
    pallas_call x1, Pallas kernels: 72.9 us -> 71.2 us  [per_device(): pl.pallas_call(functools.partial(step_kernel, n, width), out_shape=(jax.S...]
where the time goes in v4:
time: 76.1 us; the launch traced here: 75.8 us
  Pallas kernels  73.4 us (96%)
  between operations  2.38 us (3%)
    pallas_call x1, Pallas kernels, per_device(): pl.pallas_call(functools.partial(step_kernel, n, width), out_shape=(jax.S...  71.2 us
    pallas_call x1, Pallas kernels, per_device(): pl.pallas_call(hand_over, out_shape=tuple((jax.ShapeDtypeStruct(g.shape,...  2.27 us

profile of v4, /device:TPU:0, one launch (start us, length us, event | category | flops | bytes accessed | tf_op | source)
XLA Modules:
  0.0 75.8 jit_solution(13470801817467770757)
XLA Ops:
  0.6 71.2 %shard_map.129 = (f32[1,1]{1,0:T(1,128)}, f32[64,1536]{1,0:T(8,128)}, f32[64,1536]{1,0:T(8,128)}, f32[96,1024]{1,0:T(8,128)}) custom-call(bf16[512,1024]{1,0:T(8,128)(2,1)} %states_in.1, s32[2]{0:T(128)} %lengths.1, bf16[1024]{0:T(1024)(128)(2,1)} %norm_gain.1, bf16[1024,1536]{1,0:T(8,128)(2,1)} %w_gate_in.1, bf16[1024,1536]{1,0:T(8,128)(2,1)} %w_up_in.1, ...), custom_call_target="tpu_custom_call" | custom-call | tf_op jit(solution)/shard_map/pallas_call | solution.py:437
  71.8 2.3 %shard_map.130 = (f32[64,1536]{1,0:T(8,128)}, f32[64,1536]{1,0:T(8,128)}, f32[96,1024]{1,0:T(8,128)}) custom-call(f32[64,1536]{1,0:T(8,128)} %get-tuple-element.12.gate, f32[64,1536]{1,0:T(8,128)} %get-tuple-element.13.up, f32[96,1024]{1,0:T(8,128)} %get-tuple-element.14.down), custom_call_target="tpu_custom_call" | custom-call | tf_op jit(solution)/shard_map/pallas_call | solution.py:489
